TPU v7x, 32 devices: a whole 2x2x4 slice. The times are simulated.
32 devices in a mesh: dp: 8 (over y, x, core), own: 4 (over z).
Axes of the slice: x: 2, y: 2, z: 4, core: 2. Of those that a mesh axis runs over, the one named last changes fastest.
Arguments:
- grads: bfloat16 [8, 6, 8192, 128], P('dp', None, 'own'), may hold values from -6 to 6
- proj: bfloat16 [4, 3, 8192, 1024], P('own', None, 'dp'), may hold values from -0.0625 to 0.0625
- moment1: float32 [4, 3, 1024, 128], P('own', None, 'dp'), may hold values from -24 to 24
- moment2: float32 [4, 3, 1024, 128], P('own', None, 'dp'), may hold values from 0.05 to 5
- plan: int32 [6], replicated, may hold values from 0 to 3, as said below
Outputs:
- update: bfloat16 [6, 8192, 128], P(None, 'own')
- new_moment1: float32 [4, 3, 1024, 128], P('own', None, 'dp')
- new_moment2: float32 [4, 3, 1024, 128], P('own', None, 'dp')
Inputs may be any that keep to these rules, and one draw needn't show every extreme that they name: `plan`: no owner is named more than 3 times, and some owner is named exactly 3 times.
All inputs are finite; a program needn't handle non-finite values.
Results may differ from a plain program's by a relative error of at most 0.015.
Values may be sent and summed in bfloat16 or wider, within the bound.
A program may use at most 64 MiB of HBM per device.

v0:
```python
import functools
import jax
import jax.numpy as jnp
from jax import lax
from jax.experimental import pallas as pl
from jax.experimental.pallas import tpu as pltpu
from jax.sharding import PartitionSpec as P

beta_one = 0.9
beta_two = 0.999
adam_eps = 1e-08
norm_eps = 1e-06
correct_one = 1.0 - 0.9**10
correct_two = 1.0 - 0.999**10

CHUNKS = 4
F32 = jnp.float32
BF16 = jnp.bfloat16


def kernel(
    n, m, plan, grads, proj, m1, m2, out, m1_out, m2_out,
    own_half, pair_half, half_sum, chip_in, total, slot_out, slot_in, grad, weights,
    part, part_in, pair_sum, share_in, norms, norms_in, mixed, update, row_in, plane_in, picked,
    local_sem,
    s_pair, r_pair, s_chip, r_chip, s_slot, r_slot, s_row, r_row,
    s_part, r_part, s_share, r_share, s_norm, r_norm, s_mix, r_mix, s_mixf, r_mixf,
    s_back, r_back, s_home, r_home, s_out, r_out, s_outf, r_outf,
):
    mats = grads.shape[0]
    chips = n // 2
    piece = grads.shape[3]
    chunk = piece // CHUNKS
    cap = m1.shape[0]
    rank_rows = m1.shape[1]
    cols = m1.shape[2]
    rank = n * rank_rows
    dp = lax.axis_index("dp")
    own = lax.axis_index("own")
    core = lax.rem(dp, 2)
    chip = lax.div(dp, 2)
    other = 1 - core
    partner = (2 * chip + other, own)

    def at_chip(which):
        return (2 * which + core, own)

    def remote(src, dst, send, recv, device):
        return pltpu.make_async_remote_copy(
            src_ref=src, dst_ref=dst, send_sem=send, recv_sem=recv,
            device_id=device, device_id_type=pl.DeviceIdType.MESH,
        )

    def rows(ch):
        return pl.ds(ch * chunk, chunk)

    load_half = pltpu.make_async_copy(grads.at[:, core], own_half, local_sem.at[0])
    load_half.start()
    load_proj = pltpu.make_async_copy(proj, weights, local_sem.at[1])
    load_proj.start()

    owner = [plan[j] for j in range(mats)]
    place = []
    for j in range(mats):
        before = jnp.int32(0)
        for i in range(j):
            before = before + jnp.where(owner[i] == owner[j], 1, 0)
        place.append(owner[j] * cap + before)

    def occupant(slot):
        index = jnp.int32(0)
        valid = jnp.int32(0)
        for j in range(mats):
            here = place[j] == slot
            index = jnp.where(here, j, index)
            valid = jnp.where(here, 1, valid)
        return index, valid.astype(F32)

    barrier = pltpu.get_barrier_semaphore()
    for d in range(1, n):
        pl.semaphore_signal(
            barrier, inc=1, device_id=(lax.rem(dp + d, n), own),
            device_id_type=pl.DeviceIdType.MESH,
        )
    for d in range(1, m):
        pl.semaphore_signal(
            barrier, inc=1, device_id=(dp, lax.rem(own + d, m)),
            device_id_type=pl.DeviceIdType.MESH,
        )
    pl.semaphore_wait(barrier, n - 1 + m - 1)

    sends = []

    pair = []
    for ch in range(CHUNKS):
        c = remote(
            grads.at[:, other, :, rows(ch)], pair_half.at[:, :, rows(ch)],
            s_pair.at[ch], r_pair.at[ch], partner,
        )
        c.start()
        pair.append(c)
    load_half.wait()
    over_chips = {}
    for ch in range(CHUNKS):
        pair[ch].wait_recv()

        @pl.loop(0, mats * chips)
        def _(i):
            j = lax.div(i, chips)
            t = lax.rem(i, chips)
            half_sum[t, j, rows(ch)] = (
                own_half[j, t, rows(ch)].astype(F32) + pair_half[j, t, rows(ch)].astype(F32)
            ).astype(BF16)

        for d in range(1, chips):
            to = lax.rem(chip + d, chips)
            c = remote(
                half_sum.at[to, :, rows(ch)], chip_in.at[d - 1, :, rows(ch)],
                s_chip.at[ch, d], r_chip.at[ch, d], at_chip(to),
            )
            c.start()
            over_chips[ch, d] = c
    sends += pair + list(over_chips.values())

    to_owner = {}
    for ch in range(CHUNKS):
        for d in range(1, chips):
            over_chips[ch, d].wait_recv()

        @pl.loop(0, mats)
        def _(j):
            acc = half_sum[chip, j, rows(ch)].astype(F32)
            for d in range(1, chips):
                acc = acc + chip_in[d - 1, j, rows(ch)].astype(F32)
            total[j, rows(ch)] = acc.astype(BF16)

        for dz in list(range(1, m)) + [0]:
            to = lax.rem(own + dz, m)
            for k in range(cap):
                index, valid = occupant(to * cap + k)
                value = (total[index, rows(ch)].astype(F32) * valid).astype(BF16)
                if dz == 0:
                    slot_in[0, k, rows(ch)] = value
                else:
                    slot_out[dz - 1, k, rows(ch)] = value
            if dz > 0:
                c = remote(
                    slot_out.at[dz - 1, :, rows(ch)], slot_in.at[dz, :, rows(ch)],
                    s_slot.at[ch, dz], r_slot.at[ch, dz], (dp, to),
                )
                c.start()
                to_owner[ch, dz] = c
    sends += list(to_owner.values())

    guarded = []
    for ch in range(CHUNKS):
        for dz in range(m):
            if dz > 0:
                to_owner[ch, dz].wait_recv()
            plane = lax.rem(own + m - dz, m)
            d = lax.rem(plane + chips - chip, chips)
            c = remote(
                slot_in.at[dz, :, rows(ch)], grad.at[:, chip, rows(ch)],
                s_row.at[ch, dz], r_row.at[ch, d], at_chip(plane),
            )

            @pl.when(d != 0)
            def _():
                c.start()

            @pl.when(d == 0)
            def _():
                for k in range(cap):
                    grad[k, chip, rows(ch)] = slot_in[dz, k, rows(ch)]

            guarded.append((d, c))
    for ch in range(CHUNKS):
        for d in range(1, chips):
            remote(
                slot_in.at[0, :, rows(ch)], grad.at[:, chip, rows(ch)],
                s_row.at[ch, 0], r_row.at[ch, d], at_chip(chip),
            ).wait_recv()

    load_proj.wait()
    parts = []
    for k in range(cap):
        g = grad[k].reshape(chips * piece, cols)
        w = weights[k].reshape(chips * piece, rank)
        value = lax.dot_general(g, w, (((0,), (0,)), ((), ())), preferred_element_type=F32)
        value = value.T.astype(BF16)
        for t in range(chips):
            for s in range(2):
                at = (2 * t + s) * rank_rows
                part[s, k, t] = value[at : at + rank_rows]
        c = remote(part.at[other, k], part_in.at[k], s_part.at[k], r_part.at[k], partner)
        c.start()
        parts.append(c)
    shares = {}
    for k in range(cap):
        parts[k].wait_recv()
        for t in range(chips):
            pair_sum[k, t] = (part[core, k, t].astype(F32) + part_in[k, t].astype(F32)).astype(BF16)
        for d in range(1, chips):
            to = lax.rem(chip + d, chips)
            c = remote(
                pair_sum.at[k, to], share_in.at[k, d - 1],
                s_share.at[k, d], r_share.at[k, d], at_chip(to),
            )
            c.start()
            shares[k, d] = c
    sends += parts + list(shares.values())

    rank_half = []
    adam = []
    for k in range(cap):
        for d in range(1, chips):
            shares[k, d].wait_recv()
        value = pair_sum[k, chip].astype(F32)
        for d in range(1, chips):
            value = value + share_in[k, d - 1].astype(F32)
        first = beta_one * m1[k] + (1.0 - beta_one) * value
        second = beta_two * m2[k] + (1.0 - beta_two) * value * value
        m1_out[k] = first
        m2_out[k] = second
        step = first / correct_one / (jnp.sqrt(second / correct_two) + adam_eps)
        step = step.astype(BF16)
        wide = step.astype(F32)
        norms[k] = jnp.sum(value * value, axis=0, keepdims=True)
        norms[cap + k] = jnp.sum(wide * wide, axis=0, keepdims=True)
        rank_half.append(value.astype(BF16))
        adam.append(wide)
    across = []
    for d in range(1, n):
        c = remote(
            norms, norms_in.at[d - 1], s_norm.at[d], r_norm.at[d], (lax.rem(dp + d, n), own)
        )
        c.start()
        across.append(c)
    sends += across
    for c in across:
        c.wait_recv()
    sums = norms[...]
    for d in range(1, n):
        sums = sums + norms_in[d - 1]
    scale = []
    for k in range(cap):
        scale.append(jnp.sqrt(sums[cap + k]) / (jnp.sqrt(sums[k]) + norm_eps))
        mixed[k, dp] = (adam[k] - scale[k] * rank_half[k].astype(F32)).astype(BF16)
    mix = []
    for d in range(1, chips):
        to = lax.rem(chip + d, chips)
        c = remote(mixed.at[:, dp], mixed.at[:, dp], s_mix.at[d], r_mix.at[d], at_chip(to))
        c.start()
        mix.append(c)
    forward = []
    c = remote(mixed.at[:, dp], mixed.at[:, dp], s_mixf.at[0], r_mixf.at[0], partner)
    c.start()
    forward.append(c)
    for d in range(1, chips):
        mix[d - 1].wait_recv()
        at = 2 * lax.rem(chip + chips - d, chips) + core
        c = remote(mixed.at[:, at], mixed.at[:, at], s_mixf.at[d], r_mixf.at[d], partner)
        c.start()
        forward.append(c)
    for c in forward:
        c.wait_recv()
    sends += mix + forward

    back = {}
    for ch in range(CHUNKS):
        for k in range(cap):
            w = weights[k, :, rows(ch)].reshape(chips * chunk, rank)
            c_full = mixed[k].reshape(rank, cols)
            value = jnp.dot(w, c_full, preferred_element_type=F32)
            g = grad[k, :, rows(ch)].reshape(chips * chunk, cols).astype(F32)
            value = (value + scale[k] * g).astype(BF16)
            for t in range(chips):
                update[t, k, rows(ch)] = value[t * chunk : (t + 1) * chunk]
        for k in range(cap):
            row_in[chip, k, rows(ch)] = update[chip, k, rows(ch)]
        for d in range(1, chips):
            to = lax.rem(chip + d, chips)
            c = remote(
                update.at[to, :, rows(ch)], row_in.at[chip, :, rows(ch)],
                s_back.at[ch, d], r_back.at[ch, d], at_chip(to),
            )
            c.start()
            back[ch, d] = c
    sends += list(back.values())

    home = {}
    for ch in range(CHUNKS):
        for d in range(1, chips):
            back[ch, d].wait_recv()
        for dz in range(1, m):
            to = lax.rem(own + dz, m)
            c = remote(
                row_in.at[to, :, rows(ch)], plane_in[ch].at[own],
                s_home.at[ch, dz], r_home.at[ch, dz], (dp, to),
            )
            c.start()
            home[ch, dz] = c
        for k in range(cap):
            plane_in[ch][own, k] = row_in[own, k, rows(ch)]
    sends += list(home.values())

    gather = {}
    copies = []
    handed = {}
    for ch in range(CHUNKS):
        for dz in range(1, m):
            home[ch, dz].wait_recv()
        for j in range(mats):
            slot = place[j]
            picked[j, rows(ch)] = plane_in[ch][lax.div(slot, cap), lax.rem(slot, cap)]
        for d in range(1, chips):
            to = lax.rem(chip + d, chips)
            c = remote(
                picked.at[:, rows(ch)], out.at[:, core, chip, rows(ch)],
                s_out.at[ch, d], r_out.at[ch, d], at_chip(to),
            )
            c.start()
            gather[ch, d] = c
        c = remote(
            picked.at[:, rows(ch)], out.at[:, core, chip, rows(ch)],
            s_outf.at[ch, 0], r_outf.at[ch, 0], partner,
        )
        c.start()
        handed[ch, 0] = c
        c = pltpu.make_async_copy(
            picked.at[:, rows(ch)], out.at[:, core, chip, rows(ch)], local_sem.at[2 + ch]
        )
        c.start()
        copies.append(c)
    for ch in range(CHUNKS):
        for d in range(1, chips):
            gather[ch, d].wait_recv()
            source = lax.rem(chip + chips - d, chips)
            block = out.at[:, core, source, rows(ch)]
            c = remote(block, block, s_outf.at[ch, d], r_outf.at[ch, d], partner)
            c.start()
            handed[ch, d] = c
    for c in handed.values():
        c.wait_recv()
    sends += list(gather.values()) + list(handed.values())
    for c in copies:
        c.wait()
    for c in sends:
        c.wait_send()
    for d, c in guarded:

        @pl.when(d != 0)
        def _():
            c.wait_send()


def local(grads, proj, moment1, moment2, plan):
    n = lax.axis_size("dp")
    m = lax.axis_size("own")
    chips = n // 2
    mats, own_rows, cols = grads.shape[1:]
    cap, held_rows, rank = proj.shape[1:]
    rank_rows = moment1.shape[2]
    piece = held_rows // chips
    g = grads.reshape(mats, 2, chips, piece, cols)
    w = proj.reshape(cap, chips, piece, rank)
    vmem = pl.BlockSpec(memory_space=pltpu.VMEM)
    anywhere = pl.BlockSpec(memory_space=pl.ANY)
    dma = pltpu.SemaphoreType.DMA
    ch = CHUNKS
    share = (cap, rank_rows, cols)
    update, first, second = pl.pallas_call(
        functools.partial(kernel, n, m),
        out_shape=(
            jax.ShapeDtypeStruct(g.shape, BF16),
            jax.ShapeDtypeStruct(share, F32),
            jax.ShapeDtypeStruct(share, F32),
        ),
        in_specs=[pl.BlockSpec(memory_space=pltpu.SMEM), anywhere, anywhere, vmem, vmem],
        out_specs=(anywhere, vmem, vmem),
        scratch_shapes=[
            pltpu.VMEM((mats, chips, piece, cols), BF16),
            pltpu.VMEM((mats, chips, piece, cols), BF16),
            pltpu.VMEM((chips, mats, piece, cols), BF16),
            pltpu.VMEM((chips - 1, mats, piece, cols), BF16),
            pltpu.VMEM((mats, piece, cols), BF16),
            pltpu.VMEM((m - 1, cap, piece, cols), BF16),
            pltpu.VMEM((m, cap, piece, cols), BF16),
            pltpu.VMEM((cap, chips, piece, cols), BF16),
            pltpu.VMEM((cap, chips, piece, rank), BF16),
            pltpu.VMEM((2, cap, chips, rank_rows, cols), BF16),
            pltpu.VMEM((cap, chips, rank_rows, cols), BF16),
            pltpu.VMEM((cap, chips, rank_rows, cols), BF16),
            pltpu.VMEM((cap, chips - 1, rank_rows, cols), BF16),
            pltpu.VMEM((2 * cap, 1, cols), F32),
            pltpu.VMEM((n - 1, 2 * cap, 1, cols), F32),
            pltpu.VMEM((cap, n, rank_rows, cols), BF16),
            pltpu.VMEM((chips, cap, piece, cols), BF16),
            pltpu.VMEM((chips, cap, piece, cols), BF16),
            [pltpu.VMEM((m, cap, piece // ch, cols), BF16)] * ch,
            pltpu.VMEM((mats, piece, cols), BF16),
            dma((2 + ch,)),
            dma((ch,)), dma((ch,)),
            dma((ch, chips)), dma((ch, chips)),
            dma((ch, m)), dma((ch, m)),
            dma((ch, m)), dma((ch, chips)),
            dma((cap,)), dma((cap,)),
            dma((cap, chips)), dma((cap, chips)),
            dma((n,)), dma((n,)),
            dma((chips,)), dma((chips,)),
            dma((chips,)), dma((chips,)),
            dma((ch, chips)), dma((ch, chips)),
            dma((ch, m)), dma((ch, m)),
            dma((ch, chips)), dma((ch, chips)),
            dma((ch, chips)), dma((ch, chips)),
        ],
        compiler_params=pltpu.CompilerParams(collective_id=0, has_side_effects=True),
    )(plan, g, w, moment1[0], moment2[0])
    return (update.reshape(mats, own_rows, cols), first[None], second[None])


def solution(mesh):
    return jax.shard_map(
        local,
        mesh=mesh,
        in_specs=(
            P("dp", None, "own", None),
            P("own", None, "dp", None),
            P("own", None, "dp", None),
            P("own", None, "dp", None),
            P(),
        ),
        out_specs=(P(None, "own", None), P("own", None, "dp", None), P("own", None, "dp", None)),
        check_vma=False,
    )
```

profile of v0, /device:TPU:0, one launch (start us, length us, event | category | flops | bytes accessed | tf_op | source)
XLA Modules:
  0.0 99.0 jit_solution(4341712727418386320)
XLA Ops:
  0.6 93.2 %shard_map.76 = (bf16[6,2,4,256,128]{4,3,2,1,0:T(8,128)(2,1)}, f32[3,128,128]{2,1,0:T(8,128)}, f32[3,128,128]{2,1,0:T(8,128)}) custom-call(s32[6]{0:T(128)} %plan.1, bf16[6,2,4,256,128]{4,3,2,1,0:T(8,128)(2,1)} %bitcast.8, bf16[3,4,256,1024]{3,2,1,0:T(8,128)(2,1)} %bitcast.7, f32[3,128,128]{2,1,0:T(8,128)} %bitcast.12, f32[3,128,128]{2,1,0:T(8,128)} %bitcast.13), custom_call_target="tpu_custom_call" | custom-call | tf_op jit(solution)/shard_map/pallas_call | solution.py:372
  93.8 0.0 copy-start.1
  93.8 0.0 copy-start
  93.8 3.8 %copy.11 = bf16[6,2048,128]{2,1,0:T(8,128)(2,1)} copy(bf16[6,2048,128]{2,1,0:T(8,128)(2,1)} %bitcast.9) | data formatting | bytes 6291456
  97.6 0.0 copy-done.1
  97.6 0.7 copy.12
  98.3 0.0 copy-done
  98.3 0.7 copy.13
Async XLA Ops:
  93.8 3.8 %copy-start.1 = (f32[3,128,128]{2,1,0:T(8,128)S(1)}, f32[3,128,128]{2,1,0:T(8,128)}, u32[]{:S(2)}) copy-start(f32[3,128,128]{2,1,0:T(8,128)} %get-tuple-element.7) | copy-start | bytes 589828
  93.8 4.5 %copy-start = (f32[3,128,128]{2,1,0:T(8,128)S(1)}, f32[3,128,128]{2,1,0:T(8,128)}, u32[]{:S(2)}) copy-start(f32[3,128,128]{2,1,0:T(8,128)} %get-tuple-element.8) | copy-start | bytes 589828
where the time goes:
time: 100 us; the launch traced here: 99 us
  Pallas kernels  93.2 us (93%)
  local copies, waits for them, and re-layouts  5.17 us (5%)
    pallas_call x1, Pallas kernels, local(): pl.pallas_call(functools.partial(kernel, n, m), out_shape=(jax.ShapeDtype...  93.2 us
    unnamed x7, local copies, waits for them, and re-layouts  5.17 us

commit v1 on v0

v1 whole, which is shorter than its diff:
```python
import functools
import jax
import jax.numpy as jnp
from jax import lax
from jax.experimental import pallas as pl
from jax.experimental.pallas import tpu as pltpu
from jax.sharding import PartitionSpec as P

beta_one = 0.9
beta_two = 0.999
adam_eps = 1e-08
norm_eps = 1e-06
correct_one = 1.0 - 0.9**10
correct_two = 1.0 - 0.999**10

CH = 4
CB = 4
F32 = jnp.float32
BF16 = jnp.bfloat16


def rank_ranges(mats, m, cap):
    lo, hi = [mats] * cap, [0] * cap

    def walk(counts, left):
        if len(counts) == cap:
            if left == 0 and counts[-1] >= 1:
                at = 0
                for k, c in enumerate(counts):
                    lo[k] = min(lo[k], at)
                    at += c
                    hi[k] = max(hi[k], at)
            return
        for c in range(min(left, counts[-1] if counts else m), -1, -1):
            walk(counts + [c], left - c)

    walk([], mats)
    return lo, hi


def groups_of(mats, m, cap):
    lo, hi = rank_ranges(mats, m, cap)
    ranks = [[k for k in range(cap) if lo[k] <= q < hi[k]] for q in range(mats)]
    scatter = [(0, hi[0], [k for k in range(cap) if hi[k] <= hi[0]])]
    if hi[0] < mats:
        scatter.append((hi[0], mats, [k for k in range(cap) if hi[k] > hi[0]]))
    gather = []
    for k in range(cap):
        qs = [q for q in range(mats) if max(ranks[q]) == k]
        if qs:
            gather.append((qs[0], qs[-1] + 1, k))
    return ranks, scatter, gather


def plan_scalars(plan, mats):
    owner = [plan[j] for j in range(mats)]
    rank = []
    for j in range(mats):
        before = jnp.int32(0)
        for i in range(j):
            before = before + jnp.where(owner[i] == owner[j], 1, 0)
        rank.append(before)
    key = [rank[j] * mats + j for j in range(mats)]
    pos = []
    for j in range(mats):
        before = jnp.int32(0)
        for i in range(mats):
            if i != j:
                before = before + jnp.where(key[i] < key[j], 1, 0)
        pos.append(before)
    return owner, rank, pos


def kernel(n, m, plan, grads, proj, m1, m2, gat, m1_out, m2_out, sc):
    mats, chips, piece, cols = grads.shape[0], n // 2, grads.shape[3], grads.shape[4]
    cap, rank_rows = m1.shape[0], m1.shape[1]
    rank = n * rank_rows
    wide = 2
    deep = chips // wide
    ranks, scatter, gather = groups_of(mats, m, cap)
    dp = lax.axis_index("dp")
    own = lax.axis_index("own")
    core = lax.rem(dp, 2)
    chip = lax.div(dp, 2)
    xa = lax.rem(chip, wide)
    yb = lax.div(chip, wide)
    other = 1 - core
    partner = (2 * chip + other, own)
    step_f = piece // CH
    step_b = piece // CB

    def at_chip(which):
        return (2 * which + core, own)

    def remote(src, dst, send, recv, device):
        return pltpu.make_async_remote_copy(
            src_ref=src, dst_ref=dst, send_sem=send, recv_sem=recv,
            device_id=device, device_id_type=pl.DeviceIdType.MESH,
        )

    def taken(block, recv):
        remote(block, block, sc["s_pair"].at[0], recv, partner).wait_recv()

    def sent(block, send):
        remote(block, block, send, sc["r_pair"].at[0], partner).wait_send()

    def peers(axis):
        if axis == 0:
            return [(1, 1 - xa, at_chip(wide * yb + 1 - xa))]
        out = []
        for d in range(1, deep):
            y = lax.rem(yb + d, deep)
            out.append((d, y, at_chip(wide * y + xa)))
        return out

    def rows(ch):
        return pl.ds(ch * step_f, step_f)

    def rows_b(ch):
        return pl.ds(ch * step_b, step_b)

    loads = []
    for ch in range(CH):
        c = pltpu.make_async_copy(grads.at[:, core, :, rows(ch)], sc["own_half"][ch], sc["l_own"].at[ch])
        c.start()
        loads.append(c)
    load_proj = pltpu.make_async_copy(proj, sc["weights"], sc["l_rest"].at[0])
    load_proj.start()
    load_m1 = pltpu.make_async_copy(m1, sc["m1"], sc["l_rest"].at[1])
    load_m1.start()
    load_m2 = pltpu.make_async_copy(m2, sc["m2"], sc["l_rest"].at[2])
    load_m2.start()

    barrier = pltpu.get_barrier_semaphore()
    everyone = [(lax.rem(dp + d, n), own) for d in range(1, n)]
    everyone += [(dp, lax.rem(own + dz, m)) for dz in range(1, m)]
    for device in everyone:
        pl.semaphore_signal(barrier, inc=1, device_id=device, device_id_type=pl.DeviceIdType.MESH)
    for d in range(chips):

        @pl.when(jnp.logical_and(chip != own, d != chip))
        def _():
            pl.semaphore_signal(barrier, inc=1, device_id=(2 * d + core, chip), device_id_type=pl.DeviceIdType.MESH)

    owner, rank_of, pos = plan_scalars(plan, mats)
    order, owner_at, rank_at = [], [], []
    for q in range(mats):
        index = jnp.int32(0)
        who = jnp.int32(0)
        which = jnp.int32(0)
        for j in range(mats):
            here = pos[j] == q
            index = jnp.where(here, j, index)
            who = jnp.where(here, owner[j], who)
            which = jnp.where(here, rank_of[j], which)
        order.append(index)
        owner_at.append(who)
        rank_at.append(which)

    slots = {}
    for dz in range(m):
        to = lax.rem(own + dz, m)
        for k in range(cap):
            index = jnp.int32(0)
            valid = jnp.int32(0)
            for j in range(mats):
                here = jnp.logical_and(owner[j] == to, rank_of[j] == k)
                index = jnp.where(here, pos[j], index)
                valid = jnp.where(here, 1, valid)
            slots[dz, k] = (index, valid.astype(F32))

    pl.semaphore_wait(barrier, n - 1 + m - 1 + jnp.where(chip != own, m - 1, 0))

    sends = []

    pair = []
    for ch in range(CH):
        c = remote(
            grads.at[:, other, :, rows(ch)], sc["pair_half"][ch], sc["s_pair"].at[0], sc["r_pair"].at[ch], partner
        )
        c.start()
        pair.append(c)

    live = {}

    def first_sum(g, ch):
        q0, q1, _ = scatter[g]
        if g == 0:
            pair[ch].wait_recv()
            loads[ch].wait()
        hs = sc["hs"][g][ch]
        for q in range(q0, q1):
            value = sc["own_half"][ch][order[q]].astype(F32) + sc["pair_half"][ch][order[q]].astype(F32)
            value = value.astype(BF16)
            for t in range(chips):
                hs[t // wide, t % wide, q - q0] = value[t]
        axis = ch % 2
        out = []
        for d, index, device in peers(axis):
            c = remote(
                hs.at[:, index] if axis == 0 else hs.at[index], sc["r1"][g][ch].at[d - 1],
                sc["s_rs1"].at[g, ch, d - 1], sc["r_rs1"].at[g, ch, d - 1], device,
            )
            c.start()
            out.append(c)
        live["rs1", g, ch] = out

    def second_sum(g, ch):
        axis = ch % 2
        out = live["rs1", g, ch]
        for c in out:
            c.wait_recv()
        hs, r1, s1 = sc["hs"][g][ch], sc["r1"][g][ch], sc["s1"][g][ch]
        for i in range(deep if axis == 0 else wide):
            value = (hs[i, xa] if axis == 0 else hs[yb, i]).astype(F32)
            for c in range(len(out)):
                value = value + r1[c, i].astype(F32)
            s1[i] = value.astype(BF16)
        nxt = []
        for d, index, device in peers(1 - axis):
            c = remote(
                s1.at[index], sc["r2"][g][ch].at[d - 1], sc["s_rs2"].at[g, ch, d - 1], sc["r_rs2"].at[g, ch, d - 1], device
            )
            c.start()
            nxt.append(c)
        live["rs2", g, ch] = nxt
        sends.extend(out + nxt)

    def third_sum(g, ch):
        q0, q1, ready = scatter[g]
        axis = ch % 2
        out = live["rs2", g, ch]
        for c in out:
            c.wait_recv()
        s1, r2, total = sc["s1"][g][ch], sc["r2"][g][ch], sc["total"][ch]
        mine = yb if axis == 0 else xa
        value = s1[mine].astype(F32)
        for c in range(len(out)):
            value = value + r2[c].astype(F32)
        total[q0:q1] = value.astype(BF16)
        ship(ready[0], ch)
        if ch == CH - 1:
            for k in ready[1:]:
                for c in range(CH):
                    ship(k, c)

    def ship(k, ch):
        grad, slot_out = sc["grad"], sc["slot_out"]
        for dz in list(range(1, m)) + [0]:
            to = lax.rem(own + dz, m)
            index, valid = slots[dz, k]
            slot_out[k, ch, dz] = (sc["total"][ch][index].astype(F32) * valid).astype(BF16)
            c = remote(
                slot_out.at[k, ch, dz], grad.at[k, chip, rows(ch)],
                sc["s_slot"].at[1 if dz else 0], sc["r_slot"].at[k, chip], (2 * own + core, to),
            )
            if dz == 0:

                @pl.when(chip != own)
                def _():
                    c.start()

                @pl.when(chip == own)
                def _():
                    grad[k, chip, rows(ch)] = slot_out[k, ch, 0]

            else:
                c.start()

    def project(k):
        grad = sc["grad"]
        for d in range(chips):

            @pl.when(jnp.logical_or(d != chip, chip != own))
            def _():
                taken(grad.at[k, d], sc["r_slot"].at[k, d])

        if k == 0:
            load_proj.wait()
        g = grad[k].reshape(chips * piece, cols)
        w = sc["weights"][k].reshape(chips * piece, rank)
        value = lax.dot_general(g, w, (((0,), (0,)), ((), ())), preferred_element_type=F32)
        value = value.T.astype(BF16)
        part = sc["part"]
        for t in range(chips):
            for s in range(2):
                at = (2 * t + s) * rank_rows
                part[s, k, t] = value[at : at + rank_rows]
        c = remote(part.at[other, k], sc["part_in"].at[k], sc["s_part"].at[k], sc["r_part"].at[k], partner)
        c.start()
        sends.append(c)
        live["part", k] = c

    def share(k):
        live["part", k].wait_recv()
        part, part_in, pair_sum = sc["part"], sc["part_in"], sc["pair_sum"]
        for t in range(chips):
            pair_sum[k, t] = (part[core, k, t].astype(F32) + part_in[k, t].astype(F32)).astype(BF16)
        for d in range(1, chips):
            to = lax.rem(chip + d, chips)
            c = remote(
                pair_sum.at[k, to], sc["share_in"].at[k, d - 1],
                sc["s_share"].at[k], sc["r_share"].at[k], at_chip(to),
            )
            c.start()

    def adam(k):
        taken(sc["share_in"].at[k], sc["r_share"].at[k])
        if k == 0:
            load_m1.wait()
            load_m2.wait()
        value = sc["pair_sum"][k, chip].astype(F32)
        for d in range(1, chips):
            value = value + sc["share_in"][k, d - 1].astype(F32)
        first = beta_one * sc["m1"][k] + (1.0 - beta_one) * value
        second = beta_two * sc["m2"][k] + (1.0 - beta_two) * value * value
        m1_out[k] = first
        m2_out[k] = second
        step = first / correct_one / (jnp.sqrt(second / correct_two) + adam_eps)
        both = sc["both"]
        both[k, dp, 0] = step.astype(BF16)
        both[k, dp, 1] = value.astype(BF16)
        out = []
        for d in range(1, chips):
            to = lax.rem(chip + d, chips)
            c = remote(both.at[k, dp], both.at[k, dp], sc["s_mix"].at[k], sc["r_mix"].at[k, d - 1], at_chip(to))
            c.start()
            out.append(c)
        c = remote(both.at[k, dp], both.at[k, dp], sc["s_mixf"].at[k], sc["r_mixf"].at[k], partner)
        c.start()
        live["mix", k] = out

    def pass_on(k):
        both = sc["both"]
        out = live["mix", k]
        for d in range(1, chips):
            out[d - 1].wait_recv()
            at = 2 * lax.rem(chip + chips - d, chips) + core
            c = remote(both.at[k, at], both.at[k, at], sc["s_mixf"].at[k], sc["r_mixf"].at[k], partner)
            c.start()

    def back(k):
        taken(sc["both"].at[k, pl.ds(0, chips)], sc["r_mixf"].at[k])
        both, update, row_in = sc["both"], sc["update"], sc["row_in"]
        steps = both[k, :, 0].reshape(rank, cols).astype(F32)
        half = both[k, :, 1].reshape(rank, cols).astype(F32)
        step_norm = jnp.sqrt(jnp.sum(steps * steps, axis=0, keepdims=True))
        grad_norm = jnp.sqrt(jnp.sum(half * half, axis=0, keepdims=True))
        scale = step_norm / (grad_norm + norm_eps)
        sc["mixed"][...] = (steps - scale * half).astype(BF16)
        for ch in range(CB):
            w = sc["weights"][k, :, rows_b(ch)].reshape(chips * step_b, rank)
            value = jnp.dot(w, sc["mixed"][...], preferred_element_type=F32)
            g = sc["grad"][k, :, rows_b(ch)].reshape(chips * step_b, cols).astype(F32)
            value = (value + scale * g).astype(BF16)
            for t in range(chips):
                update[k, t, rows_b(ch)] = value[t * step_b : (t + 1) * step_b]
            for d in range(1, chips):
                to = lax.rem(chip + d, chips)
                c = remote(
                    update.at[k, to, rows_b(ch)], row_in.at[k, chip, rows_b(ch)],
                    sc["s_back"].at[k], sc["r_back"].at[k, ch], at_chip(to),
                )
                c.start()
            row_in[k, chip, rows_b(ch)] = update[k, chip, rows_b(ch)]

    def home(k, ch):
        row_in, plane_in = sc["row_in"], sc["plane_in"][k][ch]
        taken(row_in.at[k, pl.ds(0, chips - 1), rows_b(ch)], sc["r_back"].at[k, ch])
        for dz in range(1, m):
            to = lax.rem(own + dz, m)
            c = remote(
                row_in.at[k, to, rows_b(ch)], plane_in.at[own],
                sc["s_home"].at[k], sc["r_home"].at[k, ch], (dp, to),
            )
            c.start()
        plane_in[own] = row_in[k, own, rows_b(ch)]

    def pick(g, ch):
        q0, q1, last = gather[g]
        for k in range(last + 1):
            if (k, ch) not in live:
                live[k, ch] = True
                taken(sc["plane_in"][k][ch].at[pl.ds(0, m - 1)], sc["r_home"].at[k, ch])
        for q in range(q0, q1):
            value = sc["plane_in"][ranks[q][0]][ch][owner_at[q]]
            for k in ranks[q][1:]:
                here = (rank_at[q] == k).astype(F32)
                value = (
                    value.astype(F32) * (1.0 - here) + sc["plane_in"][k][ch][owner_at[q]].astype(F32) * here
                ).astype(BF16)
            gat[core, yb, xa, q, rows_b(ch)] = value
        block = gat.at[core, yb, xa, pl.ds(q0, q1 - q0), rows_b(ch)]
        out = []
        for d, _, device in peers(ch % 2):
            c = remote(block, block, sc["s_ag1"].at[g, ch, d - 1], sc["r_ag1"].at[g, ch, d - 1], device)
            c.start()
            out.append(c)
        live["ag1", g, ch] = out

    def spread(g, ch):
        q0, q1, _ = gather[g]
        qs = pl.ds(q0, q1 - q0)
        axis = ch % 2
        out = live["ag1", g, ch]
        for c in out:
            c.wait_recv()
        block = gat.at[core, yb, :, qs, rows_b(ch)] if axis == 0 else gat.at[core, :, xa, qs, rows_b(ch)]
        nxt = []
        for d, _, device in peers(1 - axis):
            c = remote(block, block, sc["s_ag2"].at[g, ch, d - 1], sc["r_ag2"].at[g, ch, d - 1], device)
            c.start()
            nxt.append(c)
        c = remote(block, block, sc["s_agp"].at[g], sc["r_agp"].at[g], partner)
        c.start()
        live["ag2", g, ch] = nxt
        sends.extend(out)

    def hand(g, ch):
        q0, q1, _ = gather[g]
        qs = pl.ds(q0, q1 - q0)
        axis = ch % 2
        for i, c in enumerate(live["ag2", g, ch]):
            c.wait_recv()
            d = i + 1
            if axis == 0:
                block = gat.at[core, lax.rem(yb + deep - d, deep), :, qs, rows_b(ch)]
            else:
                block = gat.at[core, :, 1 - xa, qs, rows_b(ch)]
            f = remote(block, block, sc["s_agp"].at[g], sc["r_agp"].at[g], partner)
            f.start()
        sends.extend(live["ag2", g, ch])

    events = []
    for g in range(len(scatter)):
        for ch in range(CH):
            events.append((1.5 + 0.4 * ch if g == 0 else 6.7 + 2.8 * (ch // 2) + 0.1 * ch, first_sum, (g, ch)))
            events.append(((6.3 if g == 0 else 11.1) + 2.8 * (ch // 2) + 0.1 * ch, second_sum, (g, ch)))
            events.append(((10.8 if g == 0 else 15.5) + 1.9 * (ch // 2) + 0.1 * ch, third_sum, (g, ch)))
    middle = [
        (project, (21.0, 27.5, 32.0)), (share, (22.5, 28.8, 33.3)), (adam, (26.5, 33.2, 38.0)),
        (pass_on, (32.5, 39.0, 44.5)), (back, (33.7, 40.2, 45.7)),
    ]
    leave, arrive = (38.0, 44.0, 50.0), (43.5, 49.5, 55.5)
    for k in range(cap):
        for step, times in middle:
            events.append((times[k], step, (k,)))
        for ch in range(CB):
            events.append((leave[k] + 0.7 * ch, home, (k, ch)))
    for g in range(len(gather)):
        base = arrive[gather[g][2]]
        for ch in range(CB):
            events.append((base + 1.3 * ch, pick, (g, ch)))
            events.append((base + 3.2 + 1.3 * ch, spread, (g, ch)))
            events.append((base + 6.5 + 1.3 * ch, hand, (g, ch)))
    for _, step, args in sorted(events, key=lambda e: e[0]):
        step(*args)
    for g, (q0, q1, _) in enumerate(gather):
        taken(gat.at[other, :, :, pl.ds(q0, q1 - q0)], sc["r_agp"].at[g])
    for c in sends:
        c.wait_send()
    sent(grads.at[:, other], sc["s_pair"].at[0])
    sent(sc["slot_out"].at[:, :, pl.ds(1, m - 1)], sc["s_slot"].at[1])

    @pl.when(chip != own)
    def _():
        sent(sc["slot_out"].at[:, :, 0], sc["s_slot"].at[0])

    for k in range(cap):
        sent(sc["share_in"].at[k], sc["s_share"].at[k])
        sent(sc["both"].at[k, pl.ds(0, chips - 1)], sc["s_mix"].at[k])
        sent(sc["both"].at[k, pl.ds(0, chips)], sc["s_mixf"].at[k])
        sent(sc["update"].at[k, pl.ds(0, chips - 1)], sc["s_back"].at[k])
        sent(sc["row_in"].at[k, pl.ds(0, m - 1)], sc["s_home"].at[k])
    for g, (q0, q1, _) in enumerate(gather):
        sent(gat.at[core, :, :, pl.ds(q0, q1 - q0)], sc["s_agp"].at[g])


def place(plan, gat, first, second, out, m1_out, m2_out, sem):
    mats = out.shape[0]
    _, _, pos = plan_scalars(plan, mats)
    copies = []
    for j in range(mats):
        copies.append(pltpu.make_async_copy(gat.at[:, :, :, pos[j]], out.at[j], sem.at[j]))
    copies.append(pltpu.make_async_copy(first, m1_out, sem.at[mats]))
    copies.append(pltpu.make_async_copy(second, m2_out, sem.at[mats + 1]))
    for c in copies:
        c.start()
    for c in copies:
        c.wait()


def local(grads, proj, moment1, moment2, plan):
    n = lax.axis_size("dp")
    m = lax.axis_size("own")
    chips = n // 2
    wide, deep = 2, chips // 2
    mats, own_rows, cols = grads.shape[1:]
    cap, held_rows, rank = proj.shape[1:]
    rank_rows = moment1.shape[2]
    piece = held_rows // chips
    assert chips == m
    g = grads.reshape(mats, 2, chips, piece, cols)
    w = proj.reshape(cap, chips, piece, rank)
    vmem = pl.BlockSpec(memory_space=pltpu.VMEM)
    smem = pl.BlockSpec(memory_space=pltpu.SMEM)
    anywhere = pl.BlockSpec(memory_space=pl.ANY)
    dma = pltpu.SemaphoreType.DMA
    _, scatter, gather = groups_of(mats, m, cap)
    rf, rb = piece // CH, piece // CB
    share_shape = (cap, rank_rows, cols)

    def half(*shape):
        return pltpu.VMEM(shape, BF16)

    def first_axis(ch):
        return (1, deep) if ch % 2 == 0 else (deep - 1, wide)

    sizes = [q1 - q0 for q0, q1, _ in scatter]
    sg, gg = len(scatter), len(gather)
    hops = max(1, deep - 1)
    scratch = dict(
        own_half=[half(mats, chips, rf, cols)] * CH,
        pair_half=[half(mats, chips, rf, cols)] * CH,
        hs=[[half(deep, wide, p, rf, cols)] * CH for p in sizes],
        r1=[[half(*first_axis(ch), p, rf, cols) for ch in range(CH)] for p in sizes],
        s1=[[half(first_axis(ch)[1], p, rf, cols) for ch in range(CH)] for p in sizes],
        r2=[[half(deep - 1 if ch % 2 == 0 else 1, p, rf, cols) for ch in range(CH)] for p in sizes],
        total=[half(mats, rf, cols)] * CH,
        slot_out=half(cap, CH, m, rf, cols),
        grad=half(cap, chips, piece, cols),
        weights=half(cap, chips, piece, rank),
        m1=pltpu.VMEM(share_shape, F32),
        m2=pltpu.VMEM(share_shape, F32),
        part=half(2, cap, chips, rank_rows, cols),
        part_in=half(cap, chips, rank_rows, cols),
        pair_sum=half(cap, chips, rank_rows, cols),
        share_in=half(cap, chips - 1, rank_rows, cols),
        both=half(cap, n, 2, rank_rows, cols),
        mixed=half(rank, cols),
        update=half(cap, chips, piece, cols),
        row_in=half(cap, chips, piece, cols),
        plane_in=[[half(m, rb, cols)] * CB for _ in range(cap)],
        l_own=dma((CH,)), l_rest=dma((3,)),
        s_pair=dma((1,)), r_pair=dma((CH,)),
        s_rs1=dma((sg, CH, hops)), r_rs1=dma((sg, CH, hops)),
        s_rs2=dma((sg, CH, hops)), r_rs2=dma((sg, CH, hops)),
        s_slot=dma((2,)), r_slot=dma((cap, chips)),
        s_part=dma((cap,)), r_part=dma((cap,)),
        s_share=dma((cap,)), r_share=dma((cap,)),
        s_mix=dma((cap,)), r_mix=dma((cap, chips - 1)),
        s_mixf=dma((cap,)), r_mixf=dma((cap,)),
        s_back=dma((cap,)), r_back=dma((cap, CB)),
        s_home=dma((cap,)), r_home=dma((cap, CB)),
        s_ag1=dma((gg, CB, hops)), r_ag1=dma((gg, CB, hops)),
        s_ag2=dma((gg, CB, hops)), r_ag2=dma((gg, CB, hops)),
        s_agp=dma((gg,)), r_agp=dma((gg,)),
    )
    gathered, first, second = pl.pallas_call(
        functools.partial(kernel, n, m),
        out_shape=(
            pltpu.VMEM((2, deep, wide, mats, piece, cols), BF16),
            pltpu.VMEM(share_shape, F32),
            pltpu.VMEM(share_shape, F32),
        ),
        in_specs=[smem] + [anywhere] * 4,
        out_specs=(vmem, vmem, vmem),
        scratch_shapes=[scratch],
        compiler_params=pltpu.CompilerParams(collective_id=0, has_side_effects=True),
    )(plan, g, w, moment1[0], moment2[0])
    stay = functools.partial(pltpu.with_memory_space_constraint, memory_space=pltpu.VMEM)
    update, first, second = pl.pallas_call(
        place,
        out_shape=(
            jax.ShapeDtypeStruct((mats, 2, deep, wide, piece, cols), BF16),
            jax.ShapeDtypeStruct(share_shape, F32),
            jax.ShapeDtypeStruct(share_shape, F32),
        ),
        in_specs=[smem, vmem, vmem, vmem],
        out_specs=(anywhere,) * 3,
        scratch_shapes=[dma((mats + 2,))],
    )(plan, stay(gathered), stay(first), stay(second))
    return (update.reshape(mats, own_rows, cols), first[None], second[None])


def solution(mesh):
    return jax.shard_map(
        local,
        mesh=mesh,
        in_specs=(
            P("dp", None, "own", None),
            P("own", None, "dp", None),
            P("own", None, "dp", None),
            P("own", None, "dp", None),
            P(),
        ),
        out_specs=(P(None, "own", None), P("own", None, "dp", None), P("own", None, "dp", None)),
        check_vma=False,
    )
```

time: 100 us -> 85.8 us (0.86)
  Pallas kernels: 93.2 us -> 85 us
  local copies, waits for them, and re-layouts: 5.17 us -> 0 us
    pallas_call x1 -> x2, Pallas kernels: 93.2 us -> 85 us  [the longest x1 82.5 us: local(): pl.pallas_call(functools.partial(kernel, n, m), out_shape=(pltpu.VMEM((2,...]
    unnamed x7 -> x0, local copies, waits for them, and re-layouts: 5.17 us -> none
where the time goes in v1:
time: 85.8 us; the launch traced here: 85.6 us
  Pallas kernels  85 us (99%)
    pallas_call x1, Pallas kernels, local(): pl.pallas_call(functools.partial(kernel, n, m), out_shape=(pltpu.VMEM((2,...  82.5 us
    pallas_call x1, Pallas kernels, local(): pl.pallas_call(place, out_shape=(jax.ShapeDtypeStruct((mats, 2, deep, wid...  2.51 us

profile of v1, /device:TPU:0, one launch (start us, length us, event | category | flops | bytes accessed | tf_op | source)
XLA Modules:
  0.0 85.6 jit_solution(2366179116497223342)
XLA Ops:
  0.6 82.5 %shard_map.76 = (bf16[2,2,2,6,256,128]{5,4,3,2,1,0:T(8,128)(2,1)S(1)}, f32[3,128,128]{2,1,0:T(8,128)S(1)}, f32[3,128,128]{2,1,0:T(8,128)S(1)}) custom-call(s32[6]{0:T(128)} %plan.3, bf16[6,2,4,256,128]{4,3,2,1,0:T(8,128)(2,1)} %bitcast.8, bf16[3,4,256,1024]{3,2,1,0:T(8,128)(2,1)} %bitcast.7, f32[3,128,128]{2,1,0:T(8,128)} %bitcast.9, f32[3,128,128]{2,1,0:T(8,128)} %bitcast.10), custom_call_target="tpu_custom_call" | custom-call | tf_op jit(solution)/shard_map/pallas_call | solution.py:559
  83.1 2.5 %shard_map.77 = (bf16[6,2,2,2,256,128]{5,4,3,2,1,0:T(8,128)(2,1)}, f32[3,128,128]{2,1,0:T(8,128)}, f32[3,128,128]{2,1,0:T(8,128)}) custom-call(s32[6]{0:T(128)} %plan.3, bf16[2,2,2,6,256,128]{5,4,3,2,1,0:T(8,128)(2,1)S(1)} %get-tuple-element.9.gat, f32[3,128,128]{2,1,0:T(8,128)S(1)} %get-tuple-element.10.first, f32[3,128,128]{2,1,0:T(8,128)S(1)} %get-tuple-element.11.second), custom_call_target="tpu_custom_call" | custom-call | tf_op jit(solution)/shard_map/pallas_call | solution.py:572
